TPU v7x, 32 devices: a whole 2x2x4 slice. The times are simulated.
32 devices in a mesh: seg: 4 (over y, core), sec: 8 (over z, x).
Axes of the slice: x: 2, y: 2, z: 4, core: 2. Of those that a mesh axis runs over, the one named last changes fastest.
Arguments:
- wavefunction: bfloat16 [4, 8, 256, 256], P('seg'), may hold values from -6 to 6
- left_env: bfloat16 [4, 32, 8, 256, 256], P('seg', 'sec'), may hold values from -0.375 to 0.375
- right_env: bfloat16 [4, 32, 8, 256, 256], P('seg', 'sec'), may hold values from -0.375 to 0.375
- block_sizes: int32 [4, 8], P('seg'), may hold values from 64 to 256, as said below
Outputs:
- new_wavefunction: bfloat16 [4, 8, 256, 256], P('seg')
- incoming_left_env: bfloat16 [4, 32, 8, 256, 256], P('seg', 'sec')
- incoming_right_env: bfloat16 [4, 32, 8, 256, 256], P('seg', 'sec')
Inputs may be any that keep to these rules, and one draw needn't show every extreme that they name: `block_sizes`: every block size is a multiple of 64; some block has size 256.
All inputs are finite; a program needn't handle non-finite values.
Results may differ from a plain program's by a relative error of at most 0.035.
Values may be sent and summed in bfloat16 or wider, within the bound.
No kernel may reach another device: no remote copies, remote signals or barrier semaphores. Data moves between devices by JAX's collectives and lax.ppermute only.
A program may use at most 64 MiB of HBM per device.

v0:
```python
import jax
import jax.numpy as jnp
from jax import lax
from jax.sharding import PartitionSpec as P

ITERS = 4
epsilon = 1e-06


def passed_along(block, axis, distance):
    devices = range(lax.axis_size(axis))
    route = [(i - distance, i) for i in devices if i - distance in devices]
    return lax.ppermute(block, axis, route)


def body(wavefunction, left_env, right_env, block_sizes):
    left_local = left_env[0]
    right_local = right_env[0]
    blocks = left_local.shape[3]
    groups = lax.axis_size("sec")
    channels = left_local.shape[0] * groups
    sizes = block_sizes[0]
    index = jnp.arange(blocks)
    live = (index[:, None] < sizes[None, :]).astype(jnp.float32)
    mask = live[:, :, None] * jnp.transpose(live)[None, :, :]
    start = jnp.transpose(wavefunction[0], (1, 0, 2)).astype(jnp.float32) * mask
    state_tensor = (start / jnp.sqrt(jnp.mean(start * start) + epsilon)).astype(jnp.bfloat16)
    root_channels = jnp.sqrt(jnp.float32(channels))
    for iteration in range(ITERS):
        state_f = state_tensor.astype(jnp.float32)
        product = jnp.einsum(
            "wkab,bkc->wkac", left_local, state_tensor, preferred_element_type=jnp.float32
        ).astype(jnp.bfloat16)
        applied = (
            lax.psum(
                jnp.einsum(
                    "wkac,wkcd->akd", product, right_local, preferred_element_type=jnp.float32
                ).astype(jnp.bfloat16),
                "sec",
            ).astype(jnp.float32)
            / root_channels
        )
        theta = jnp.sum(state_f * applied) / jnp.sum(state_f * state_f)
        update = mask * (state_f - (applied - theta * state_f))
        state_tensor = (update / jnp.sqrt(jnp.mean(update * update) + epsilon)).astype(jnp.bfloat16)
    scale_factor = jnp.sqrt(jnp.float32(blocks))
    left_portion = jnp.einsum(
        "akc,wkab->wkcb", state_tensor, left_local, preferred_element_type=jnp.float32
    ).astype(jnp.bfloat16)
    built_left = (
        jnp.einsum("gxah,hxe->gxae", left_portion, state_tensor, preferred_element_type=jnp.float32)
        / scale_factor
    ).astype(jnp.bfloat16)
    incoming_left_env = passed_along(built_left[None], "seg", 1)
    right_portion = jnp.einsum(
        "akc,wkcd->wkad", state_tensor, right_local, preferred_element_type=jnp.float32
    ).astype(jnp.bfloat16)
    built_right = (
        jnp.einsum(
            "njpq,tjq->njpt", right_portion, state_tensor, preferred_element_type=jnp.float32
        )
        / scale_factor
    ).astype(jnp.bfloat16)
    incoming_right_env = passed_along(built_right[None], "seg", -1)
    new_wave = jnp.transpose(state_tensor, (1, 0, 2))[None]
    return (new_wave, incoming_left_env, incoming_right_env)


def solution(mesh):
    placed = (
        P("seg", None, None, None),
        P("seg", "sec", None, None, None),
        P("seg", "sec", None, None, None),
        P("seg", None),
    )
    return jax.shard_map(
        body,
        mesh=mesh,
        in_specs=placed,
        out_specs=(
            P("seg", None, None, None),
            P("seg", "sec", None, None, None),
            P("seg", "sec", None, None, None),
        ),
        check_vma=False,
    )
```

profile of v0, /device:TPU:1, one launch (start us, length us, event | category | flops | bytes accessed | tf_op | source)
XLA Modules:
  0.0 461.6 jit_solution(12130565121797320660)
XLA Ops:
  7.2 0.7 fusion.133
  7.9 0.7 fusion.132
  8.7 2.5 fusion.66
  11.8 7.3 %fusion.92 = bf16[256,8,256]{2,0,1:T(8,128)(2,1)} fusion(bf16[1,4,8,256,256]{4,3,2,1,0:T(8,128)(2,1)} %param.6, bf16[1,4,8,256,256]{4,3,2,1,0:T(8,128)(2,1)} %param.5, bf16[1,8,256,256]{3,2,1,0:T(8,128)(2,1)} %param.4, f32[]{:T(128)S(6)} %sqrt.15, f32[8,256]{1,0:T(8,128)S(1)} %fusion.133, f32[256,8]{0,1:T(8,128)S(1)} %fusion.132), kind=kOutput, calls=%fused_computation.92 | convolution fusion | flops 2152726528 | bytes 10502148 | tf_op jit(solution)/shard_map/wkac,wkcd->akd/dot_general | solution.py:36
  19.2 80.3 %all-reduce.5.cloned.1.call-done = bf16[256,8,256]{2,0,1:T(8,128)(2,1)} async-done(((bf16[256,8,256]{2,0,1:T(8,128)(2,1)}), bf16[256,8,256]{2,0,1:T(8,128)(2,1)}) %all-reduce.5.cloned.1.call-update) | async-done | bytes 1048592 | tf_op jit(solution)/shard_map/psum | solution.py:35
  99.5 2.9 fusion.53
  103.7 1.7 multiply_reduce_fusion.3
  106.1 0.8 divide_convert_fusion.3
  106.9 6.8 %fusion.99 = bf16[256,8,256]{2,0,1:T(8,128)(2,1)} fusion(bf16[256,8,256]{2,0,1:T(8,128)(2,1)S(1)} %divide_convert_fusion.3, bf16[1,4,8,256,256]{4,3,2,1,0:T(8,128)(2,1)} %param.6, bf16[1,4,8,256,256]{4,3,2,1,0:T(8,128)(2,1)} %param.5), kind=kOutput, calls=%fused_computation.93 | convolution fusion | flops 2150105088 | bytes 10485760 | tf_op jit(solution)/shard_map/wkac,wkcd->akd/dot_general | solution.py:36
  113.8 0.2 all-reduce.9.cloned.1.call-start
  114.0 77.8 %all-reduce.7.cloned.1.call-done = bf16[256,8,256]{2,0,1:T(8,128)(2,1)} async-done(((bf16[256,8,256]{2,0,1:T(8,128)(2,1)}), bf16[256,8,256]{2,0,1:T(8,128)(2,1)}) %all-reduce.7.cloned.1.call-update) | async-done | bytes 1048592 | tf_op jit(solution)/shard_map/psum | solution.py:35
  191.8 2.5 fusion.56
  195.6 1.5 multiply_reduce_fusion.2
  197.8 0.7 divide_convert_fusion.2
  198.5 6.8 %fusion.106 = bf16[256,8,256]{2,0,1:T(8,128)(2,1)} fusion(bf16[256,8,256]{2,0,1:T(8,128)(2,1)S(1)} %divide_convert_fusion.2, bf16[1,4,8,256,256]{4,3,2,1,0:T(8,128)(2,1)} %param.6, bf16[1,4,8,256,256]{4,3,2,1,0:T(8,128)(2,1)} %param.5), kind=kOutput, calls=%fused_computation.94 | convolution fusion | flops 2150105088 | bytes 10485760 | tf_op jit(solution)/shard_map/wkac,wkcd->akd/dot_general | solution.py:36
  205.3 77.8 %all-reduce.9.cloned.1.call-done = bf16[256,8,256]{2,0,1:T(8,128)(2,1)} async-done(((bf16[256,8,256]{2,0,1:T(8,128)(2,1)}), bf16[256,8,256]{2,0,1:T(8,128)(2,1)}) %all-reduce.9.cloned.1.call-update) | async-done | bytes 1048592 | tf_op jit(solution)/shard_map/psum | solution.py:35
  283.2 2.5 fusion.59
  287.0 1.5 multiply_reduce_fusion.1
  289.2 0.7 divide_convert_fusion.1
  289.9 6.8 %fusion.113 = bf16[256,8,256]{2,0,1:T(8,128)(2,1)} fusion(bf16[256,8,256]{2,0,1:T(8,128)(2,1)S(1)} %divide_convert_fusion.1, bf16[1,4,8,256,256]{4,3,2,1,0:T(8,128)(2,1)} %param.6, bf16[1,4,8,256,256]{4,3,2,1,0:T(8,128)(2,1)} %param.5), kind=kOutput, calls=%fused_computation.95 | convolution fusion | flops 2150105088 | bytes 10485760 | tf_op jit(solution)/shard_map/wkac,wkcd->akd/dot_general | solution.py:36
  296.7 78.0 %all-reduce.11.cloned.1.call-done = bf16[256,8,256]{2,0,1:T(8,128)(2,1)} async-done(((bf16[256,8,256]{2,0,1:T(8,128)(2,1)}), bf16[256,8,256]{2,0,1:T(8,128)(2,1)}) %all-reduce.11.cloned.1.call-update) | async-done | bytes 1048592 | tf_op jit(solution)/shard_map/psum | solution.py:35
  374.7 2.5 fusion.62
  378.5 1.5 multiply_reduce_fusion
  380.7 0.7 divide_convert_fusion
  381.4 7.1 %fusion = bf16[1,4,8,256,256]{3,4,1,2,0:T(8,128)(2,1)} fusion(bf16[256,8,256]{2,0,1:T(8,128)(2,1)S(1)} %divide_convert_fusion, bf16[1,4,8,256,256]{4,3,2,1,0:T(8,128)(2,1)} %param.5), kind=kOutput, calls=%fused_computation.7 | convolution fusion | flops 2153775104 | bytes 9437184 | tf_op jit(solution)/shard_map/gxah,hxe->gxae/dot_general | solution.py:51
  388.5 3.7 collective-permute-start
  392.2 6.5 %fusion.1 = bf16[1,4,8,256,256]{3,4,1,2,0:T(8,128)(2,1)} fusion(bf16[256,8,256]{2,0,1:T(8,128)(2,1)S(1)} %divide_convert_fusion, bf16[1,4,8,256,256]{4,3,2,1,0:T(8,128)(2,1)} %param.6), kind=kOutput, calls=%fused_computation.8 | convolution fusion | flops 2153775104 | bytes 9437184 | tf_op jit(solution)/shard_map/njpq,tjq->njpt/dot_general | solution.py:59
  398.7 2.5 collective-permute-start.1
  401.3 36.7 %collective-permute-done = bf16[1,4,8,256,256]{3,4,1,2,0:T(8,128)(2,1)} collective-permute-done((bf16[1,4,8,256,256]{3,4,1,2,0:T(8,128)(2,1)}, bf16[1,4,8,256,256]{3,4,1,2,0:T(8,128)(2,1)}, u32[]{:S(2)}, u32[]{:S(2)}) %collective-permute-start) | collective-permute-done | bytes 4194336 | tf_op jit(solution)/shard_map/ppermute | solution.py:13
  438.0 6.2 %copy.12 = bf16[1,4,8,256,256]{4,3,2,1,0:T(8,128)(2,1)} copy(bf16[1,4,8,256,256]{3,4,1,2,0:T(8,128)(2,1)} %collective-permute-done) | data formatting | bytes 8388608
  444.1 4.7 %collective-permute-done.1 = bf16[1,4,8,256,256]{3,4,1,2,0:T(8,128)(2,1)} collective-permute-done((bf16[1,4,8,256,256]{3,4,1,2,0:T(8,128)(2,1)}, bf16[1,4,8,256,256]{3,4,1,2,0:T(8,128)(2,1)}, u32[]{:S(2)}, u32[]{:S(2)}) %collective-permute-start.1) | collective-permute-done | bytes 4194336 | tf_op jit(solution)/shard_map/ppermute | solution.py:13
  448.9 6.2 %copy.13 = bf16[1,4,8,256,256]{4,3,2,1,0:T(8,128)(2,1)} copy(bf16[1,4,8,256,256]{3,4,1,2,0:T(8,128)(2,1)} %collective-permute-done.1) | data formatting | bytes 8388608
  (19 shorter events, 0.2 us)
Async XLA Ops:
  7.2 92.3 %all-reduce.5.cloned.1.call-start = ((), (), s32[]{:S(2)}) async-start(), calls=%async_computation | async-start | bytes 2097152 | tf_op jit(solution)/shard_map/psum | solution.py:35
  11.8 87.6 %copy-start = (bf16[1,8,256,256]{3,2,1,0:T(8,128)(2,1)S(1)}, bf16[1,8,256,256]{3,2,1,0:T(8,128)(2,1)}, u32[]{:S(2)}) copy-start(bf16[1,8,256,256]{3,2,1,0:T(8,128)(2,1)} %param.4) | copy-start | bytes 3145732
  19.1 172.6 %all-reduce.7.cloned.1.call-start = ((), (), s32[]{:S(2)}) async-start(), calls=%async_computation.1 | async-start | bytes 2097152 | tf_op jit(solution)/shard_map/psum | solution.py:35
  99.5 4.2 copy-start.1
  113.8 169.4 %all-reduce.9.cloned.1.call-start = ((), (), s32[]{:S(2)}) async-start(), calls=%async_computation.2 | async-start | bytes 2097152 | tf_op jit(solution)/shard_map/psum | solution.py:35
  191.8 3.8 copy-start.3
  205.3 169.4 %all-reduce.11.cloned.1.call-start = ((), (), s32[]{:S(2)}) async-start(), calls=%async_computation.3 | async-start | bytes 2097152 | tf_op jit(solution)/shard_map/psum | solution.py:35
  283.2 3.8 copy-start.4
  374.7 3.8 copy-start.2
  381.4 10.8 %copy-start.5 = (bf16[256,8,256]{2,0,1:T(8,128)(2,1)}, bf16[256,8,256]{2,0,1:T(8,128)(2,1)S(1)}, u32[]{:S(2)}) copy-start(bf16[256,8,256]{2,0,1:T(8,128)(2,1)S(1)} %divide_convert_fusion) | copy-start | bytes 3145732
  388.5 49.5 %collective-permute-start = (bf16[1,4,8,256,256]{3,4,1,2,0:T(8,128)(2,1)}, bf16[1,4,8,256,256]{3,4,1,2,0:T(8,128)(2,1)}, u32[]{:S(2)}, u32[]{:S(2)}) collective-permute-start(bf16[1,4,8,256,256]{3,4,1,2,0:T(8,128)(2,1)} %fusion), channel_id=1, source_target_pairs={{0,8},{8,16},{16,24},{1,9},{9,17},{17,25},{2,10},{10,18},{18,26},{... | collective-permute-start | bytes 12582920 | tf_op jit(solution)/shard_map/ppermute | solution.py:13
  398.7 50.1 %collective-permute-start.1 = (bf16[1,4,8,256,256]{3,4,1,2,0:T(8,128)(2,1)}, bf16[1,4,8,256,256]{3,4,1,2,0:T(8,128)(2,1)}, u32[]{:S(2)}, u32[]{:S(2)}) collective-permute-start(bf16[1,4,8,256,256]{3,4,1,2,0:T(8,128)(2,1)} %fusion.1), channel_id=1, source_target_pairs={{8,0},{16,8},{24,16},{9,1},{17,9},{25,17},{10,2},{18,10},{26,18},{... | collective-permute-start | bytes 12582920 | tf_op jit(solution)/shard_map/ppermute | solution.py:13
Sparse Core Ops, SparseCore 0:
  19.3 80.1 all-reduce.4
  113.9 77.8 all-reduce.6
  205.4 77.7 all-reduce.8
  296.8 77.8 all-reduce.10
where the time goes:
time: 462 us
  waiting for transfers between devices  355 us (77%)
  matrix products  41.2 us (9%)
  other arithmetic  23.3 us (5%)
  between operations  22.7 us (5%)
  local copies, waits for them, and re-layouts  12.4 us (3%)
  starting transfers between devices  6.56 us (1%)
    psum x4, waiting for transfers between devices, body(): lax.psum(jnp.einsum('wkac,wkcd->akd', product, right_local, preferred_ele...  314 us
    ppermute x2, waiting for transfers between devices, passed_along(): return lax.ppermute(block, axis, route)  41.4 us
    dot_general x4, matrix products, body(): jnp.einsum('wkac,wkcd->akd', product, right_local, preferred_element_type...  27.6 us
    unnamed x14, local copies, waits for them, and re-layouts  12.4 us
    reduce_sum x4, other arithmetic, body(): theta = jnp.sum(state_f * applied) / jnp.sum(state_f * state_f)  10.3 us
  transfers between devices with their start and end apart: 6, of which 6 were waited for; matrix products, arithmetic and copies ran while one was open for 3% of the time, Pallas kernels for 0%

commit v1 on v0

--- a/solution.py
+++ b/solution.py
@@ -32,11 +32,14 @@
             "wkab,bkc->wkac", left_local, state_tensor, preferred_element_type=jnp.float32
         ).astype(jnp.bfloat16)
         applied = (
-            lax.psum(
-                jnp.einsum(
-                    "wkac,wkcd->akd", product, right_local, preferred_element_type=jnp.float32
-                ).astype(jnp.bfloat16),
-                "sec",
+            jnp.sum(
+                lax.all_gather(
+                    jnp.einsum(
+                        "wkac,wkcd->akd", product, right_local, preferred_element_type=jnp.float32
+                    ).astype(jnp.bfloat16),
+                    "sec",
+                ),
+                axis=0,
             ).astype(jnp.float32)
             / root_channels
         )

time: 462 us -> 677 us (1.47)
  waiting for transfers between devices: 355 us -> 532 us
  other arithmetic: 23.3 us -> 57.3 us
    all_gather x0 -> x4, waiting for transfers between devices: none -> 494 us  [body(): lax.all_gather(jnp.einsum('wkac,wkcd->akd', product, right_local, preferr...]
    psum x4 -> x0, waiting for transfers between devices: 314 us -> none  [body(): lax.psum(jnp.einsum('wkac,wkcd->akd', product, right_local, preferred_ele...]
    reduce_sum x0 -> x4, other arithmetic: none -> 22.1 us  [body(): jnp.sum(lax.all_gather(jnp.einsum('wkac,wkcd->akd', product, right_local,...]
where the time goes in v1:
time: 677 us; the launch traced here: 676 us
  waiting for transfers between devices  532 us (79%)
  other arithmetic  57.3 us (8%)
  matrix products  45.6 us (7%)
  between operations  22.7 us (3%)
  local copies, waits for them, and re-layouts  12.4 us (2%)
  starting transfers between devices  6.84 us (1%)
    all_gather x4, waiting for transfers between devices, body(): lax.all_gather(jnp.einsum('wkac,wkcd->akd', product, right_local, preferr...  494 us
    ppermute x2, waiting for transfers between devices, passed_along(): return lax.ppermute(block, axis, route)  37.5 us
    dot_general x4, matrix products, body(): jnp.einsum('wkac,wkcd->akd', product, right_local, preferred_element_type...  28.5 us
    reduce_sum x4, other arithmetic, body(): jnp.sum(lax.all_gather(jnp.einsum('wkac,wkcd->akd', product, right_local,...  22.1 us
  transfers between devices with their start and end apart: 6, of which 6 were waited for; matrix products, arithmetic and copies ran while one was open for 3% of the time, Pallas kernels for 0%

profile of v1, /device:TPU:1, one launch (start us, length us, event | category | flops | bytes accessed | tf_op | source)
XLA Modules:
  0.0 676.5 jit_solution(15733584605304724718)
XLA Ops:
  8.7 2.5 fusion.58
  11.8 7.2 %fusion.106 = bf16[256,8,256]{2,0,1:T(8,128)(2,1)} fusion(bf16[1,4,8,256,256]{4,3,2,1,0:T(8,128)(2,1)} %param.6, bf16[1,4,8,256,256]{4,3,2,1,0:T(8,128)(2,1)} %param.5, bf16[1,8,256,256]{3,2,1,0:T(8,128)(2,1)} %param.4, f32[]{:T(128)S(6)} %sqrt.15, f32[8,256]{1,0:T(8,128)S(1)} %fusion.147, f32[256,8]{0,1:T(8,128)S(1)} %fusion.148), kind=kOutput, calls=%fused_computation.119 | convolution fusion | flops 2152726528 | bytes 10502148 | tf_op jit(solution)/shard_map/wkac,wkcd->akd/dot_general | solution.py:37
  19.1 125.9 %all-gather.9.cloned.1.call-done = bf16[2048,8,256]{2,0,1:T(8,128)(2,1)} async-done(((bf16[256,8,256]{2,0,1:T(8,128)(2,1)}), bf16[2048,8,256]{2,0,1:T(8,128)(2,1)}) %all-gather.9.cloned.1.call-update) | async-done | bytes 8388624 | tf_op jit(solution)/shard_map/all_gather | solution.py:36
  145.0 5.0 reduce_sum.166
  150.0 1.5 fusion.61
  152.9 1.7 multiply_reduce_fusion.3
  156.2 7.1 %fusion.113 = bf16[256,8,256]{2,0,1:T(8,128)(2,1)} fusion(bf16[256,8,256]{2,0,1:T(8,128)(2,1)S(1)} %divide_convert_fusion.3, bf16[1,4,8,256,256]{4,3,2,1,0:T(8,128)(2,1)} %param.6, bf16[1,4,8,256,256]{4,3,2,1,0:T(8,128)(2,1)} %param.5), kind=kOutput, calls=%fused_computation.120 | convolution fusion | flops 2150105088 | bytes 10485760 | tf_op jit(solution)/shard_map/wkac,wkcd->akd/dot_general | solution.py:37
  163.6 122.6 %all-gather.11.cloned.1.call-done = bf16[2048,8,256]{2,0,1:T(8,128)(2,1)} async-done(((bf16[256,8,256]{2,0,1:T(8,128)(2,1)}), bf16[2048,8,256]{2,0,1:T(8,128)(2,1)}) %all-gather.11.cloned.1.call-update) | async-done | bytes 8388624 | tf_op jit(solution)/shard_map/all_gather | solution.py:36
  286.1 4.9 reduce_sum.170
  291.1 2.4 fusion.64
  294.8 2.8 multiply_reduce_fusion.2
  298.2 2.9 divide_convert_fusion.2
  301.1 7.1 %fusion.120 = bf16[256,8,256]{2,0,1:T(8,128)(2,1)} fusion(bf16[256,8,256]{2,0,1:T(8,128)(2,1)} %divide_convert_fusion.2, bf16[1,4,8,256,256]{4,3,2,1,0:T(8,128)(2,1)} %param.6, bf16[1,4,8,256,256]{4,3,2,1,0:T(8,128)(2,1)} %param.5), kind=kOutput, calls=%fused_computation.121 | convolution fusion | flops 2150105088 | bytes 10485760 | tf_op jit(solution)/shard_map/wkac,wkcd->akd/dot_general | solution.py:37
  308.2 122.7 %all-gather.13.cloned.1.call-done = bf16[2048,8,256]{2,0,1:T(8,128)(2,1)} async-done(((bf16[256,8,256]{2,0,1:T(8,128)(2,1)}), bf16[2048,8,256]{2,0,1:T(8,128)(2,1)}) %all-gather.13.cloned.1.call-update) | async-done | bytes 8388624 | tf_op jit(solution)/shard_map/all_gather | solution.py:36
  431.0 6.1 reduce_sum.174
  437.1 2.8 fusion.67
  441.2 3.1 multiply_reduce_fusion.1
  445.0 3.2 divide_convert_fusion.1
  448.1 7.1 %fusion.127 = bf16[256,8,256]{2,0,1:T(8,128)(2,1)} fusion(bf16[256,8,256]{2,0,1:T(8,128)(2,1)} %divide_convert_fusion.1, bf16[1,4,8,256,256]{4,3,2,1,0:T(8,128)(2,1)} %param.6, bf16[1,4,8,256,256]{4,3,2,1,0:T(8,128)(2,1)} %param.5), kind=kOutput, calls=%fused_computation.122 | convolution fusion | flops 2150105088 | bytes 10485760 | tf_op jit(solution)/shard_map/wkac,wkcd->akd/dot_general | solution.py:37
  455.3 122.8 %all-gather.15.cloned.1.call-done = bf16[2048,8,256]{2,0,1:T(8,128)(2,1)} async-done(((bf16[256,8,256]{2,0,1:T(8,128)(2,1)}), bf16[2048,8,256]{2,0,1:T(8,128)(2,1)}) %all-gather.15.cloned.1.call-update) | async-done | bytes 8388624 | tf_op jit(solution)/shard_map/all_gather | solution.py:36
  578.1 6.2 reduce_sum.178
  584.2 2.8 fusion.70
  588.4 3.1 multiply_reduce_fusion
  592.1 9.0 %fusion = bf16[1,4,8,256,256]{3,4,1,2,0:T(8,128)(2,1)} fusion(bf16[256,8,256]{2,0,1:T(8,128)(2,1)} %reduce_sum.178, bf16[256,8,256]{2,0,1:T(8,128)(2,1)} %divide_convert_fusion.1, f32[]{:T(128)S(6)} %sqrt.19, f32[]{:T(128)S(6)} %div.139, f32[8,256]{1,0:T(8,128)S(1)} %fusion.147, f32[256,8]{0,1:T(8,128)S(1)} %fusion.148, bf16[1,4,8,256,256]{4,3,2,1,0:T(8,128)(2,1)} %param.5), kind=kOutput, calls=%fused_computation.12 | convolution fusion | flops 2164260864 | bytes 10502152 | tf_op jit(solution)/shard_map/gxah,hxe->gxae/dot_general | solution.py:54
  601.1 4.4 collective-permute-start
  605.5 8.1 %fusion.1 = bf16[1,4,8,256,256]{3,4,1,2,0:T(8,128)(2,1)} fusion(bf16[256,8,256]{2,0,1:T(8,128)(2,1)} %reduce_sum.178, bf16[256,8,256]{2,0,1:T(8,128)(2,1)} %divide_convert_fusion.1, f32[]{:T(128)S(6)} %sqrt.19, f32[]{:T(128)S(6)} %div.139, f32[8,256]{1,0:T(8,128)S(1)} %fusion.147, f32[256,8]{0,1:T(8,128)S(1)} %fusion.148, bf16[1,4,8,256,256]{4,3,2,1,0:T(8,128)(2,1)} %param.6), kind=kOutput, calls=%fused_computation.13 | convolution fusion | flops 2164260864 | bytes 10502152 | tf_op jit(solution)/shard_map/njpq,tjq->njpt/dot_general | solution.py:62
  613.6 2.1 collective-permute-start.1
  615.8 4.3 fusion.146
  620.1 31.2 %collective-permute-done = bf16[1,4,8,256,256]{3,4,1,2,0:T(8,128)(2,1)} collective-permute-done((bf16[1,4,8,256,256]{3,4,1,2,0:T(8,128)(2,1)}, bf16[1,4,8,256,256]{3,4,1,2,0:T(8,128)(2,1)}, u32[]{:S(2)}, u32[]{:S(2)}) %collective-permute-start) | collective-permute-done | bytes 4194336 | tf_op jit(solution)/shard_map/ppermute | solution.py:13
  651.3 6.2 copy.12
  657.4 6.3 collective-permute-done.1
  663.8 6.2 copy.13
  (15 shorter events, 2.7 us)
Async XLA Ops:
  7.2 137.9 %all-gather.9.cloned.1.call-start = ((), (), s32[]{:S(2)}) async-start(), calls=%async_computation | async-start | bytes 9437184 | tf_op jit(solution)/shard_map/all_gather | solution.py:36
  19.1 267.1 %all-gather.11.cloned.1.call-start = ((), (), s32[]{:S(2)}) async-start(), calls=%async_computation.1 | async-start | bytes 9437184 | tf_op jit(solution)/shard_map/all_gather | solution.py:36
  145.0 5.0 copy-start
  156.2 7.2 %copy-start.1 = (bf16[256,8,256]{2,0,1:T(8,128)(2,1)}, bf16[256,8,256]{2,0,1:T(8,128)(2,1)S(1)}, u32[]{:S(2)}) copy-start(bf16[256,8,256]{2,0,1:T(8,128)(2,1)S(1)} %divide_convert_fusion.3) | copy-start | bytes 3145732
  163.3 267.6 %all-gather.13.cloned.1.call-start = ((), (), s32[]{:S(2)}) async-start(), calls=%async_computation.2 | async-start | bytes 9437184 | tf_op jit(solution)/shard_map/all_gather | solution.py:36
  308.2 269.9 %all-gather.15.cloned.1.call-start = ((), (), s32[]{:S(2)}) async-start(), calls=%async_computation.3 | async-start | bytes 9437184 | tf_op jit(solution)/shard_map/all_gather | solution.py:36
  601.1 50.1 %collective-permute-start = (bf16[1,4,8,256,256]{3,4,1,2,0:T(8,128)(2,1)}, bf16[1,4,8,256,256]{3,4,1,2,0:T(8,128)(2,1)}, u32[]{:S(2)}, u32[]{:S(2)}) collective-permute-start(bf16[1,4,8,256,256]{3,4,1,2,0:T(8,128)(2,1)} %fusion), channel_id=1, source_target_pairs={{0,8},{8,16},{16,24},{1,9},{9,17},{17,25},{2,10},{10,18},{18,26},{... | collective-permute-start | bytes 12582920 | tf_op jit(solution)/shard_map/ppermute | solution.py:13
  613.6 50.1 %collective-permute-start.1 = (bf16[1,4,8,256,256]{3,4,1,2,0:T(8,128)(2,1)}, bf16[1,4,8,256,256]{3,4,1,2,0:T(8,128)(2,1)}, u32[]{:S(2)}, u32[]{:S(2)}) collective-permute-start(bf16[1,4,8,256,256]{3,4,1,2,0:T(8,128)(2,1)} %fusion.1), channel_id=1, source_target_pairs={{8,0},{16,8},{24,16},{9,1},{17,9},{25,17},{10,2},{18,10},{26,18},{... | collective-permute-start | bytes 12582920 | tf_op jit(solution)/shard_map/ppermute | solution.py:13
Sparse Core Ops, SparseCore 0:
  19.2 125.7 all-gather.8
  163.5 122.6 all-gather.10
  308.3 122.6 all-gather.12
  455.4 122.6 all-gather.14
